TPU v7x, 32 devices: a whole 2x2x4 slice. The times are simulated.
32 devices in a mesh: blen: 4 (over z), tm: 8 (over y, x, core).
Axes of the slice: x: 2, y: 2, z: 4, core: 2. Of those that a mesh axis runs over, the one named last changes fastest.
Arguments:
- model_grid: bfloat16 [256, 2, 512, 512], P(('blen', 'tm')), may hold values from -6 to 6
- vis_values: float32 [2, 16384], P(None, ('blen', 'tm')), may hold values from -6 to 6
- weights: float32 [16384], P(('blen', 'tm')), may hold values from 0.3 to 3
- flags: int32 [16384], P(('blen', 'tm')), may hold values 0 or 1
- uv_frac: float32 [2, 16384], P(None, ('blen', 'tm')), may hold values from 0 to 1
- cell_offset: int32 [2, 16384], P(None, ('blen', 'tm')), may hold values from 3 to 507
- tile_index: int32 [16384, 1], P(('blen', 'tm')), may hold values from 0 to 255; in each aligned block of 512 rows (0 to 511, 512 to 1023, ...) at most 4 rows name the same one
Outputs:
- gradient: float32 [8192, 8192], P(('blen', 'tm'))
- weighted_residual: float32 [2, 16384], P(None, ('blen', 'tm'))
Inputs may be any that keep to these rules, and one draw needn't show every extreme that they name: `tile_index`: in the rows of one device no tile is named by more than 4 rows, and some device has a tile named by exactly 4 rows.
All inputs are finite; a program needn't handle non-finite values. No bound on the sum of `flags` on one device may be relied on, other than what follows from the above.
Results may differ from a plain program's by a relative error of at most 0.0095.
Values sent between devices are 32-bit elements; how exact they have to be, the bound alone decides.
No kernel may reach another device: no remote copies, remote signals or barrier semaphores. Data moves between devices by JAX's collectives and lax.ppermute only.
A program may use at most 192 MiB of HBM per device.

v0:
```python
import math
import jax
import jax.numpy as jnp
from jax import lax
from jax.sharding import PartitionSpec as P

NPIX = 8192
KSUP = 8
NT = 16
MOST = 4
kernel_scale = 0.5
highest = lax.Precision.HIGHEST


def taps_full(offsets, fractions, tile_side):
    cell_ids = lax.broadcasted_iota(jnp.int32, offsets.shape + (tile_side,), offsets.ndim)
    shifted = cell_ids - offsets[..., None]
    distance = shifted.astype(jnp.float32) - fractions[..., None]
    inside = (shifted >= 1 - KSUP // 2) & (shifted <= KSUP // 2)
    values = jnp.exp(-kernel_scale * distance * distance)
    return jnp.where(inside, values, 0.0).astype(jnp.bfloat16)


def phase_table(row_count, col_count, period):
    row_ids = lax.broadcasted_iota(jnp.int32, (row_count, col_count), 0)
    col_ids = lax.broadcasted_iota(jnp.int32, (row_count, col_count), 1)
    angles = 2.0 * math.pi / period * (row_ids * col_ids % period).astype(jnp.float32)
    return (jnp.cos(angles), jnp.sin(angles))


def complex_block(cos_part, sin_part):
    return jnp.stack([jnp.stack([cos_part, -sin_part]), jnp.stack([sin_part, cos_part])])


def on_device(model_grid, vis_values, weights, flags, uv_frac, cell_offset, tile_index):
    blen_size = lax.axis_size("blen")
    tm_size = lax.axis_size("tm")
    devices = blen_size * tm_size
    per_dev = model_grid.shape[0]
    tile_side = model_grid.shape[2]
    vis_count = weights.shape[0]
    ntiles = per_dev * devices
    total_slots = ntiles * MOST
    tile_ids = tile_index[:, 0]
    matches = tile_ids[:, None] == lax.broadcasted_iota(jnp.int32, (vis_count, ntiles), 1)
    counts = jnp.sum(matches.astype(jnp.int32), axis=0)
    starts = jnp.cumsum(counts) - counts
    sorting = jnp.argsort(tile_ids, stable=True)
    position = (
        jnp.zeros((vis_count,), jnp.int32).at[sorting].set(jnp.arange(vis_count, dtype=jnp.int32))
    )
    first_slot = jnp.sum(jnp.where(matches, starts[None, :], 0), axis=1)
    rank_in_tile = position - first_slot
    owner_dev = tile_ids // per_dev
    local_tile = tile_ids % per_dev
    slot_of = (local_tile * devices + owner_dev) * MOST + rank_in_tile
    weighted = weights * flags.astype(jnp.float32)
    float_fields = jnp.stack([vis_values[0], vis_values[1], weighted, uv_frac[0], uv_frac[1]])
    send_float = jnp.zeros((5, total_slots), jnp.float32).at[:, slot_of].set(float_fields)
    send_int = jnp.zeros((2, total_slots), jnp.int32).at[:, slot_of].set(cell_offset)
    recv_float, recv_int = (
        lax.all_to_all(
            send_float.reshape(5, per_dev, devices, MOST),
            ("blen", "tm"),
            split_axis=2,
            concat_axis=2,
            tiled=True,
        ),
        lax.all_to_all(
            send_int.reshape(2, per_dev, devices, MOST),
            ("blen", "tm"),
            split_axis=2,
            concat_axis=2,
            tiled=True,
        ),
    )
    owner_rows = devices * MOST
    block_rows = 512 if owner_rows % 512 == 0 else owner_rows
    block_count = owner_rows // block_rows
    float_blocks = recv_float.reshape(5, per_dev, block_count, block_rows).transpose(2, 0, 1, 3)
    int_blocks = recv_int.reshape(2, per_dev, block_count, block_rows).transpose(2, 0, 1, 3)

    def grid_step(adjoint, inputs):
        part_float, part_int = inputs
        taps_u = taps_full(part_int[0], part_float[3], tile_side)
        taps_v = taps_full(part_int[1], part_float[4], tile_side)
        partial_sums = jnp.einsum(
            "qrj,qcji->qrci", taps_v, model_grid, preferred_element_type=jnp.float32
        )
        predicted = jnp.sum(partial_sums * taps_u[:, :, None, :], axis=-1)
        observed = jnp.stack([part_float[0], part_float[1]], axis=-1)
        residual = part_float[2][..., None] * (predicted - observed)
        spread = (residual[..., None] * taps_u[:, :, None, :]).astype(jnp.bfloat16)
        adjoint = adjoint + jnp.einsum(
            "qrj,qrci->qcji", taps_v, spread, preferred_element_type=jnp.float32
        )
        return (adjoint, jnp.moveaxis(residual, -1, 0))

    start_adjoint = jnp.zeros((per_dev, 2, tile_side, tile_side), jnp.float32)
    adjoint, residual_blocks = lax.scan(grid_step, start_adjoint, (float_blocks, int_blocks))
    residual_slots = residual_blocks.transpose(1, 2, 0, 3).reshape(2, per_dev, owner_rows)
    returned = lax.all_to_all(
        residual_slots.reshape(2, per_dev, devices, MOST),
        ("blen", "tm"),
        split_axis=2,
        concat_axis=2,
        tiled=True,
    )
    weighted_residual = returned.reshape(2, total_slots)[:, slot_of]
    relaid = lax.all_to_all(adjoint, "tm", split_axis=2, concat_axis=0, tiled=True)
    tile_cols = NT // blen_size
    col_slice = tile_side // tm_size
    pieces = relaid.reshape(NT, tile_cols, 2, col_slice, tile_side)
    cos_small, sin_small = phase_table(NT, NT, NT)
    small_turn = complex_block(cos_small, sin_small)
    cos_twist, sin_twist = phase_table(NT, tile_side, NPIX)
    cos_tile, sin_tile = phase_table(tile_side, tile_side, tile_side)
    tile_turn = complex_block(cos_tile, sin_tile)
    section_one = jnp.einsum("acnt,tvcji->anvji", small_turn, pieces, precision=highest)
    twist_c = cos_twist[:, None, None, :]
    twist_s = sin_twist[:, None, None, :]
    turned = jnp.stack(
        [
            section_one[0] * twist_c - section_one[1] * twist_s,
            section_one[0] * twist_s + section_one[1] * twist_c,
        ]
    )
    columns = jnp.einsum("acmi,cnvji->amnvj", tile_turn, turned, precision=highest)
    rows_dev = NPIX // devices
    spread_cols = rows_dev * tile_cols * col_slice
    packed = columns.reshape(2, 1, devices, spread_cols)
    landed = lax.all_to_all(packed, ("blen", "tm"), split_axis=2, concat_axis=1, tiled=True)
    landed = landed.reshape(2, blen_size, tm_size, rows_dev, tile_cols, col_slice)
    small_split = small_turn.reshape(2, 2, NT, blen_size, tile_cols)
    section_two = jnp.einsum("acnpv,cptrvj->antrj", small_split, landed, precision=highest)
    twist_cv = cos_twist.reshape(NT, tm_size, 1, col_slice)
    twist_sv = sin_twist.reshape(NT, tm_size, 1, col_slice)
    turned_rows = jnp.stack(
        [
            section_two[0] * twist_cv - section_two[1] * twist_sv,
            section_two[0] * twist_sv + section_two[1] * twist_cv,
        ]
    )
    real_turn = jnp.stack([cos_tile, -sin_tile]).reshape(2, tile_side, tm_size, col_slice)
    image_rows = jnp.einsum("cmtj,cntrj->rmn", real_turn, turned_rows, precision=highest)
    gradient = image_rows.reshape(rows_dev, NPIX) / NPIX
    return (gradient, weighted_residual)


def solution(mesh):
    in_specs = (
        P(("blen", "tm"), None, None, None),
        P(None, ("blen", "tm")),
        P(("blen", "tm")),
        P(("blen", "tm")),
        P(None, ("blen", "tm")),
        P(None, ("blen", "tm")),
        P(("blen", "tm"), None),
    )
    out_specs = (P(("blen", "tm"), None), P(None, ("blen", "tm")))
    return jax.shard_map(
        on_device, mesh=mesh, in_specs=in_specs, out_specs=out_specs, check_vma=False
    )
```

profile of v0, /device:TPU:0, one launch (start us, length us, event | category | flops | bytes accessed | tf_op | source)
XLA Modules:
  0.0 1047.1 jit_solution(14593329809357333968)
XLA Ops:
  3.0 4.4 sort.17
  14.8 7.3 all-to-all-start.1
  27.3 3.0 all-to-all-done.1
  30.3 2.8 all-to-all-start
  33.3 7.1 all-to-all-done
  43.2 5.3 multiply_reduce_fusion
  48.5 7.2 convolution_bitcast_fusion
  55.7 25.1 %copy.78 = f32[8,2,512,512]{3,1,0,2:T(2,128)} copy(f32[8,2,512,512]{2,3,1,0:T(8,128)} %convolution_bitcast_fusion) | data formatting | bytes 33554432 | tf_op jit(solution)/shard_map/while/body/eval_jaxpr/qrj,qrci->qcji/transpose | solution.py:94
  80.8 6.0 all-to-all-start.2
  87.2 3.9 fusion.60
  91.0 4.1 fusion.58
  97.8 173.0 %all-to-all-done.2 = f32[8,2,512,512]{3,1,0,2:T(2,128)} async-done(((f32[8,2,512,512]{3,1,0,2:T(2,128)}), f32[8,2,512,512]{3,1,0,2:T(2,128)}, u32[]{:S(2)}, u32[]{:S(2)}) %all-to-all-start.2) | async-done | bytes 16777248 | tf_op jit(solution)/shard_map/all_to_all | solution.py:110
  270.8 2.6 all-to-all-start.4
  273.4 11.0 %copy.79 = f32[8,2,512,512]{3,2,1,0:T(8,128)S(1)} copy(f32[8,2,512,512]{3,1,0,2:T(2,128)} %all-to-all-done.2) | data formatting | bytes 33554432 | tf_op jit(solution)/shard_map/all_to_all | solution.py:110
  284.4 6.7 copy.80
  291.1 42.0 %fusion.11 = f32[2,16,4,64,512]{4,1,3,2,0:T(8,128)} fusion(f32[16,4,2,64,512]{4,3,2,1,0:T(8,128)} %bitcast.109, f32[1,2,16,16]{3,2,1,0:T(8,128)S(1)} %get-tuple-element.44, f32[1,2,16,16]{3,2,1,0:T(8,128)S(1)} %get-tuple-element.43), kind=kOutput, calls=%fused_computation.23 | convolution fusion | flops 1610613760 | bytes 33558528 | tf_op jit(solution)/shard_map/acnt,tvcji->anvji/dot_general | solution.py:119
  333.1 7.1 multiply_subtract_fusion.1
  340.2 6.4 pad_maximum_fusion
  346.6 67.2 %fusion.14 = f32[2,512,16,4,64]{1,4,3,2,0:T(8,128)} fusion(f32[2,16,4,64,512]{4,1,3,2,0:T(8,128)} %pad_maximum_fusion, f32[1,2,512,512]{3,2,1,0:T(8,128)S(1)} %copy-done, f32[1,2,512,512]{3,2,1,0:T(8,128)S(1)} %get-tuple-element.34), kind=kOutput, calls=%fused_computation.24 | convolution fusion | flops 51540656128 | bytes 37748736 | tf_op jit(solution)/shard_map/acmi,cnvji->amnvj/dot_general | solution.py:128
  413.8 31.1 %copy.83 = f32[2,512,16,4,64]{4,3,2,1,0:T(4,128)} copy(f32[2,512,16,4,64]{1,4,3,2,0:T(8,128)} %fusion.14) | data formatting | bytes 33554432 | tf_op jit(solution)/shard_map/acmi,cnvji->amnvj/dot_general | solution.py:128
  444.9 27.4 %reshape.436 = f32[2,1,32,65536]{3,2,0,1:T(8,128)} reshape(f32[2,512,16,4,64]{4,3,2,1,0:T(4,128)} %copy.83) | data formatting | bytes 33554432 | tf_op jit(solution)/shard_map/reshape | solution.py:131
  472.2 28.6 %copy.84 = f32[2,1,32,65536]{3,0,1,2:T(2,128)} copy(f32[2,1,32,65536]{3,2,0,1:T(8,128)} %reshape.436) | data formatting | bytes 33554432 | tf_op jit(solution)/shard_map/reshape | solution.py:131
  500.9 6.0 all-to-all-start.3
  507.1 4.2 sine_negate_fusion
  516.5 363.0 %all-to-all-done.3 = f32[2,1,32,65536]{3,0,1,2:T(2,128)} async-done(((f32[2,1,32,65536]{3,0,1,2:T(2,128)}), f32[2,1,32,65536]{3,0,1,2:T(2,128)}, u32[]{:S(2)}, u32[]{:S(2)}) %all-to-all-start.3) | async-done | bytes 16777248 | tf_op jit(solution)/shard_map/all_to_all | solution.py:132
  879.5 38.4 %reshape.487 = f32[2,4,8,256,4,64]{5,4,3,0,2,1:T(4,128)} reshape(f32[2,1,32,65536]{3,0,1,2:T(2,128)} %all-to-all-done.3) | data formatting | bytes 33554432 | tf_op jit(solution)/shard_map/reshape | solution.py:133
  918.0 30.9 %copy.86 = f32[2,4,8,256,4,64]{3,4,1,0,5,2:T(4,128)} copy(f32[2,4,8,256,4,64]{5,4,3,0,2,1:T(4,128)} %reshape.487) | data formatting | bytes 33554432 | tf_op jit(solution)/shard_map/reshape | solution.py:133
  948.8 31.8 %fusion.17 = f32[2,16,8,256,64]{3,1,4,2,0:T(8,128)S(1)} fusion(f32[2,4,8,256,4,64]{3,4,1,0,5,2:T(4,128)} %copy.86, f32[2,2,16,4,4,1,1]{2,4,3,1,6,5,0:T(4,128)S(1)} %maximum_bitcast_fusion.17), kind=kOutput, calls=%fused_computation.25 | convolution fusion | flops 1610612736 | bytes 33558528 | tf_op jit(solution)/shard_map/acnpv,cptrvj->antrj/dot_general | solution.py:135
  980.6 2.8 multiply_subtract_fusion
  985.2 42.3 %fusion.10 = f32[256,512,16]{1,0,2:T(8,128)} fusion(f32[2,16,8,256,64]{3,1,4,2,0:T(8,128)S(1)} %pad_maximum_fusion.1, f32[1,512,8,64]{1,3,2,0:T(8,128)S(1)} %get-tuple-element.56, f32[1,512,8,64]{1,3,2,0:T(8,128)S(1)} %get-tuple-element.57), kind=kOutput, calls=%fused_computation.18 | convolution fusion | flops 25772425216 | bytes 27262976 | tf_op jit(solution)/shard_map/cmtj,cntrj->rmn/dot_general | solution.py:145
  1027.6 10.3 copy.88
  1037.9 8.9 copy.92
  (60 shorter events, 28.0 us)
Async XLA Ops:
  11.4 14.1 %copy-start.1 = (s32[512]{0:T(512)}, s32[512]{0:T(512)S(1)}, u32[]{:S(2)}) copy-start(s32[512]{0:T(512)S(1)} %compare_select_fusion) | copy-start | bytes 6148
  14.8 15.5 %all-to-all-start.1 = ((s32[2,8,32,4]{1,3,0,2:T(4,128)}), s32[2,8,32,4]{1,3,0,2:T(4,128)S(1)}, u32[]{:S(2)}, u32[]{:S(2)}) async-start(s32[2,8,32,4]{1,3,0,2:T(4,128)} %copy.70), calls=%async_computation.1 | async-start | bytes 262144 | tf_op jit(solution)/shard_map/all_to_all | solution.py:69
  30.3 10.1 all-to-all-start
  80.8 190.0 %all-to-all-start.2 = ((f32[8,2,512,512]{3,1,0,2:T(2,128)}), f32[8,2,512,512]{3,1,0,2:T(2,128)}, u32[]{:S(2)}, u32[]{:S(2)}) async-start(f32[8,2,512,512]{3,1,0,2:T(2,128)} %copy.78), calls=%async_computation.2 | async-start | bytes 33554432 | tf_op jit(solution)/shard_map/all_to_all | solution.py:110
  270.8 230.0 %all-to-all-start.4 = ((f32[2,8,32,4]{1,3,0,2:T(4,128)}), f32[2,8,32,4]{1,3,0,2:T(4,128)S(1)}, u32[]{:S(2)}, u32[]{:S(2)}) async-start(f32[2,8,32,4]{1,3,0,2:T(4,128)} %copy.90), calls=%async_computation.4 | async-start | bytes 262144 | tf_op jit(solution)/shard_map/all_to_all | solution.py:102
  340.2 6.4 copy-start
  500.9 6.0 copy-start.2
  500.9 378.7 %all-to-all-start.3 = ((f32[2,1,32,65536]{3,0,1,2:T(2,128)}), f32[2,1,32,65536]{3,0,1,2:T(2,128)}, u32[]{:S(2)}, u32[]{:S(2)}) async-start(f32[2,1,32,65536]{3,0,1,2:T(2,128)} %copy.84), calls=%async_computation.3 | async-start | bytes 33554432 | tf_op jit(solution)/shard_map/all_to_all | solution.py:132
where the time goes:
time: 1060 us; the launch traced here: 1050 us
  waiting for transfers between devices  546 us (52%)
  local copies, waits for them, and re-layouts  235 us (22%)
  matrix products  196 us (18%)
  other arithmetic  44 us (4%)
  starting transfers between devices  24.7 us (2%)
    all_to_all x1, waiting for transfers between devices, on_device(): lax.all_to_all(packed, ('blen', 'tm'), split_axis=2, concat_axis=1, tiled...  363 us
    all_to_all x1, waiting for transfers between devices, on_device(): lax.all_to_all(adjoint, 'tm', split_axis=2, concat_axis=0, tiled=True)  173 us
    reshape x2, local copies, waits for them, and re-layouts, on_device(): landed.reshape(2, blen_size, tm_size, rows_dev, tile_cols, col_slice)  69.3 us
    dot_general x1, matrix products, on_device(): jnp.einsum('acmi,cnvji->amnvj', tile_turn, turned, precision=highest)  67.2 us
    reshape x2, local copies, waits for them, and re-layouts, on_device(): packed = columns.reshape(2, 1, devices, spread_cols)  56 us
    dot_general x1, matrix products, on_device(): jnp.einsum('cmtj,cntrj->rmn', real_turn, turned_rows, precision=highest)  42.3 us
    dot_general x1, matrix products, on_device(): jnp.einsum('acnt,tvcji->anvji', small_turn, pieces, precision=highest)  42 us
    dot_general x1, matrix products, on_device(): jnp.einsum('acnpv,cptrvj->antrj', small_split, landed, precision=highest)  31.8 us
  transfers between devices with their start and end apart: 5, of which 4 were waited for; matrix products, arithmetic and copies ran while one was open for 24% of the time, Pallas kernels for 0%

commit v1 on v0

--- a/solution.py
+++ b/solution.py
@@ -10,6 +10,18 @@
 MOST = 4
 kernel_scale = 0.5
 highest = lax.Precision.HIGHEST
+
+
+def in_blocks(value, dim, size):
+    shape = value.shape
+    blocks = value.reshape(*shape[:dim], size, shape[dim] // size, *shape[dim + 1 :])
+    return jnp.moveaxis(blocks, dim, 0)
+
+
+def joined_along(blocks, dim):
+    blocks = jnp.moveaxis(blocks, 0, dim)
+    shape = blocks.shape
+    return blocks.reshape(*shape[:dim], shape[dim] * shape[dim + 1], *shape[dim + 2 :])
 
 
 def taps_full(offsets, fractions, tile_side):
@@ -107,7 +119,14 @@
         tiled=True,
     )
     weighted_residual = returned.reshape(2, total_slots)[:, slot_of]
-    relaid = lax.all_to_all(adjoint, "tm", split_axis=2, concat_axis=0, tiled=True)
+    peers, mine = (lax.axis_size("tm"), lax.axis_index("tm"))
+    blocks = in_blocks(adjoint, 2, peers)
+    outs = [blocks[mine]]
+    for step in range(1, peers):
+        sent = blocks[mine ^ step]
+        outs.append(lax.ppermute(sent, "tm", [(i, i ^ step) for i in range(peers)]))
+    blocks = jnp.stack(outs)[mine ^ jnp.arange(peers)]
+    relaid = joined_along(blocks, 0)
     tile_cols = NT // blen_size
     col_slice = tile_side // tm_size
     pieces = relaid.reshape(NT, tile_cols, 2, col_slice, tile_side)

time: 1060 us -> 1050 us (level)
  waiting for transfers between devices: 546 us -> 528 us
    all_to_all x1 -> x0, waiting for transfers between devices: 173 us -> none  [on_device(): lax.all_to_all(adjoint, 'tm', split_axis=2, concat_axis=0, tiled=True)]
    ppermute x0 -> x7, waiting for transfers between devices: none -> 155 us  [on_device(): outs.append(lax.ppermute(sent, 'tm', [(i, i ^ step) for i in range(peers)]))]
    transpose x1 -> x0, local copies, waits for them, and re-layouts: 25.1 us -> none  [grid_step(): jnp.einsum('qrj,qrci->qcji', taps_v, spread, preferred_element_type=jnp.f...]
    unnamed x11 -> x16, local copies, waits for them, and re-layouts: 12.5 us -> 34.6 us
    all_to_all x2 -> x0, local copies, waits for them, and re-layouts: 17.7 us -> none  [on_device(): lax.all_to_all(adjoint, 'tm', split_axis=2, concat_axis=0, tiled=True)]
    gather x0 -> x1, local copies, waits for them, and re-layouts: none -> 13.7 us  [on_device(): blocks = jnp.stack(outs)[mine ^ jnp.arange(peers)]]
    squeeze x0 -> x1, local copies, waits for them, and re-layouts: none -> 11.1 us  [on_device(): sent = blocks[mine ^ step]]
  transfers between devices with their start and end apart: 5 -> 11, of which waited for: 4 -> 6; matrix products, arithmetic and copies ran while one was open for 24% -> 26% of each run, Pallas kernels for 0% -> 0%
where the time goes in v1:
time: 1050 us; the launch traced here: 1040 us
  waiting for transfers between devices  528 us (50%)
  local copies, waits for them, and re-layouts  243 us (23%)
  matrix products  196 us (19%)
  other arithmetic  46.2 us (4%)
  starting transfers between devices  21.1 us (2%)
    all_to_all x1, waiting for transfers between devices, on_device(): lax.all_to_all(packed, ('blen', 'tm'), split_axis=2, concat_axis=1, tiled...  363 us
    ppermute x7, waiting for transfers between devices, on_device(): outs.append(lax.ppermute(sent, 'tm', [(i, i ^ step) for i in range(peers)]))  155 us
    reshape x2, local copies, waits for them, and re-layouts, on_device(): landed.reshape(2, blen_size, tm_size, rows_dev, tile_cols, col_slice)  69.3 us
    dot_general x1, matrix products, on_device(): jnp.einsum('acmi,cnvji->amnvj', tile_turn, turned, precision=highest)  67 us
    reshape x2, local copies, waits for them, and re-layouts, on_device(): packed = columns.reshape(2, 1, devices, spread_cols)  56 us
    dot_general x1, matrix products, on_device(): jnp.einsum('cmtj,cntrj->rmn', real_turn, turned_rows, precision=highest)  42.3 us
    dot_general x1, matrix products, on_device(): jnp.einsum('acnt,tvcji->anvji', small_turn, pieces, precision=highest)  42 us
    unnamed x16, local copies, waits for them, and re-layouts  34.6 us
  transfers between devices with their start and end apart: 11, of which 6 were waited for; matrix products, arithmetic and copies ran while one was open for 26% of the time, Pallas kernels for 0%

profile of v1, /device:TPU:0, one launch (start us, length us, event | category | flops | bytes accessed | tf_op | source)
XLA Modules:
  0.0 1035.6 jit_solution(9201545138206474838)
XLA Ops:
  3.0 4.4 sort.17
  14.8 7.3 all-to-all-start.1
  33.3 7.1 all-to-all-done
  46.3 5.5 multiply_reduce_fusion
  51.8 7.3 fusion.30
  59.1 11.1 %dynamic-slice_bitcast_fusion = (f32[8,2,64,512]{3,2,1,0:T(8,128)S(1)}, f32[8,2,64,512]{3,2,1,0:T(8,128)}, f32[8,2,64,512]{3,2,1,0:T(8,128)}, f32[8,2,64,512]{3,...) fusion(f32[8,2,8,64,512]{4,3,2,1,0:T(8,128)} %bitcast.142, ...), kind=kLoop, calls=%fused_computation.53 | loop fusion | bytes 29360156 | tf_op jit(solution)/shard_map/squeeze | solution.py:126
  72.4 3.9 fusion.61
  76.9 4.1 fusion.59
  89.0 31.1 %collective-permute-done.1 = f32[8,2,64,512]{3,2,1,0:T(8,128)} collective-permute-done((f32[8,2,64,512]{3,2,1,0:T(8,128)}, f32[8,2,64,512]{3,2,1,0:T(8,128)}, u32[]{:S(2)}, u32[]{:S(2)}) %collective-permute-start.1) | collective-permute-done | bytes 2097184 | tf_op jit(solution)/shard_map/ppermute | solution.py:127
  120.1 3.2 bitcast_dynamic-update-slice_fusion.7
  129.5 34.5 %collective-permute-done.2 = f32[8,2,64,512]{3,2,1,0:T(8,128)} collective-permute-done((f32[8,2,64,512]{3,2,1,0:T(8,128)}, f32[8,2,64,512]{3,2,1,0:T(8,128)}, u32[]{:S(2)}, u32[]{:S(2)}) %collective-permute-start.2) | collective-permute-done | bytes 2097184 | tf_op jit(solution)/shard_map/ppermute | solution.py:127
  164.1 3.2 bitcast_dynamic-update-slice_fusion.4
  167.3 3.2 bitcast_dynamic-update-slice_fusion.3
  170.5 89.6 %collective-permute-done.4 = f32[8,2,64,512]{3,2,1,0:T(8,128)} collective-permute-done((f32[8,2,64,512]{3,2,1,0:T(8,128)}, f32[8,2,64,512]{3,2,1,0:T(8,128)}, u32[]{:S(2)}, u32[]{:S(2)}) %collective-permute-start.4) | collective-permute-done | bytes 2097184 | tf_op jit(solution)/shard_map/ppermute | solution.py:127
  263.2 3.2 bitcast_dynamic-update-slice_fusion.1
  267.9 13.7 %gather_fusion = f32[8,8,2,64,512]{4,3,2,1,0:T(8,128)} fusion(f32[8,8,2,64,512]{4,3,2,1,0:T(8,128)} %bitcast_dynamic-update-slice_fusion, s32[1024]{0:T(1024)S(1)} %pad_clamp_fusion.1), kind=kCustom, calls=%fused_computation | custom fusion | bytes 33554464 | tf_op jit(solution)/shard_map/gather | solution.py:128
  281.6 42.0 %fusion.11 = f32[2,16,4,64,512]{4,1,3,2,0:T(8,128)} fusion(f32[16,4,2,64,512]{4,3,2,1,0:T(8,128)} %bitcast.144, f32[1,2,16,16]{3,2,1,0:T(8,128)S(1)} %get-tuple-element.51, f32[1,2,16,16]{3,2,1,0:T(8,128)S(1)} %get-tuple-element.50), kind=kOutput, calls=%fused_computation.23 | convolution fusion | flops 1610613760 | bytes 33558528 | tf_op jit(solution)/shard_map/acnt,tvcji->anvji/dot_general | solution.py:138
  323.6 7.1 multiply_subtract_fusion.1
  330.8 6.6 pad_maximum_fusion
  337.3 67.0 %fusion.14 = f32[2,512,16,4,64]{1,4,3,2,0:T(8,128)} fusion(f32[2,16,4,64,512]{4,1,3,2,0:T(8,128)} %pad_maximum_fusion, f32[1,2,512,512]{3,2,1,0:T(8,128)S(1)} %copy-done.1, f32[1,2,512,512]{3,2,1,0:T(8,128)S(1)} %copy-done), kind=kOutput, calls=%fused_computation.24 | convolution fusion | flops 51540656128 | bytes 37748736 | tf_op jit(solution)/shard_map/acmi,cnvji->amnvj/dot_general | solution.py:147
  404.3 31.1 %copy.79 = f32[2,512,16,4,64]{4,3,2,1,0:T(4,128)} copy(f32[2,512,16,4,64]{1,4,3,2,0:T(8,128)} %fusion.14) | data formatting | bytes 33554432 | tf_op jit(solution)/shard_map/acmi,cnvji->amnvj/dot_general | solution.py:147
  435.4 27.4 %reshape.466 = f32[2,1,32,65536]{3,2,0,1:T(8,128)} reshape(f32[2,512,16,4,64]{4,3,2,1,0:T(4,128)} %copy.79) | data formatting | bytes 33554432 | tf_op jit(solution)/shard_map/reshape | solution.py:150
  462.7 28.6 %copy.80 = f32[2,1,32,65536]{3,0,1,2:T(2,128)} copy(f32[2,1,32,65536]{3,2,0,1:T(8,128)} %reshape.466) | data formatting | bytes 33554432 | tf_op jit(solution)/shard_map/reshape | solution.py:150
  491.3 3.9 all-to-all-start.2
  495.5 4.2 sine_negate_fusion
  504.9 363.1 %all-to-all-done.2 = f32[2,1,32,65536]{3,0,1,2:T(2,128)} async-done(((f32[2,1,32,65536]{3,0,1,2:T(2,128)}), f32[2,1,32,65536]{3,0,1,2:T(2,128)}, u32[]{:S(2)}, u32[]{:S(2)}) %all-to-all-start.2) | async-done | bytes 16777248 | tf_op jit(solution)/shard_map/all_to_all | solution.py:151
  868.0 38.4 %reshape.526 = f32[2,4,8,256,4,64]{5,4,3,0,2,1:T(4,128)} reshape(f32[2,1,32,65536]{3,0,1,2:T(2,128)} %all-to-all-done.2) | data formatting | bytes 33554432 | tf_op jit(solution)/shard_map/reshape | solution.py:152
  906.4 30.9 %copy.82 = f32[2,4,8,256,4,64]{3,4,1,0,5,2:T(4,128)} copy(f32[2,4,8,256,4,64]{5,4,3,0,2,1:T(4,128)} %reshape.526) | data formatting | bytes 33554432 | tf_op jit(solution)/shard_map/reshape | solution.py:152
  937.3 31.8 %fusion.17 = f32[2,16,8,256,64]{3,1,4,2,0:T(8,128)S(1)} fusion(f32[2,4,8,256,4,64]{3,4,1,0,5,2:T(4,128)} %copy.82, f32[2,2,16,4,4,1,1]{2,4,3,1,6,5,0:T(4,128)S(1)} %maximum_bitcast_fusion.17), kind=kOutput, calls=%fused_computation.25 | convolution fusion | flops 1610612736 | bytes 33558528 | tf_op jit(solution)/shard_map/acnpv,cptrvj->antrj/dot_general | solution.py:154
  973.7 42.3 %fusion.10 = f32[256,512,16]{1,0,2:T(8,128)} fusion(f32[2,16,8,256,64]{3,1,4,2,0:T(8,128)S(1)} %pad_maximum_fusion.1, f32[1,512,8,64]{1,3,2,0:T(8,128)S(1)} %get-tuple-element.63, f32[1,512,8,64]{1,3,2,0:T(8,128)S(1)} %get-tuple-element.64), kind=kOutput, calls=%fused_computation.18 | convolution fusion | flops 25772425216 | bytes 27262976 | tf_op jit(solution)/shard_map/cmtj,cntrj->rmn/dot_general | solution.py:164
  1016.0 10.3 copy.84
  1026.3 8.9 copy.88
  (80 shorter events, 58.5 us)
Async XLA Ops:
  14.8 15.5 %all-to-all-start.1 = ((s32[2,8,32,4]{1,3,0,2:T(4,128)}), s32[2,8,32,4]{1,3,0,2:T(4,128)S(1)}, u32[]{:S(2)}, u32[]{:S(2)}) async-start(s32[2,8,32,4]{1,3,0,2:T(4,128)} %copy.68), calls=%async_computation.1 | async-start | bytes 262144 | tf_op jit(solution)/shard_map/all_to_all | solution.py:81
  30.3 10.1 all-to-all-start
  70.2 14.7 %collective-permute-start = (f32[8,2,64,512]{3,2,1,0:T(8,128)}, f32[8,2,64,512]{3,2,1,0:T(8,128)}, u32[]{:S(2)}, u32[]{:S(2)}) collective-permute-start(f32[8,2,64,512]{3,2,1,0:T(8,128)} %get-tuple-element.40), channel_id=1, source_target_pairs={{0,1},{1,0},{2,3},{3,2},{4,5},{5,4},{6,7},{7,6},{8,9},{9,8},{10,11... | collective-permute-start | bytes 6291464 | tf_op jit(solution)/shard_map/ppermute | solution.py:127
  70.3 49.8 %collective-permute-start.1 = (f32[8,2,64,512]{3,2,1,0:T(8,128)}, f32[8,2,64,512]{3,2,1,0:T(8,128)}, u32[]{:S(2)}, u32[]{:S(2)}) collective-permute-start(f32[8,2,64,512]{3,2,1,0:T(8,128)} %get-tuple-element.39), channel_id=1, source_target_pairs={{0,2},{1,3},{2,0},{3,1},{4,6},{5,7},{6,4},{7,5},{8,10},{9,11},{10,... | collective-permute-start | bytes 6291464 | tf_op jit(solution)/shard_map/ppermute | solution.py:127
  70.8 93.2 %collective-permute-start.2 = (f32[8,2,64,512]{3,2,1,0:T(8,128)}, f32[8,2,64,512]{3,2,1,0:T(8,128)}, u32[]{:S(2)}, u32[]{:S(2)}) collective-permute-start(f32[8,2,64,512]{3,2,1,0:T(8,128)} %get-tuple-element.38), channel_id=1, source_target_pairs={{0,3},{1,2},{2,1},{3,0},{4,7},{5,6},{6,5},{7,4},{8,11},{9,10},{10,... | collective-permute-start | bytes 6291464 | tf_op jit(solution)/shard_map/ppermute | solution.py:127
  76.3 91.0 %collective-permute-start.3 = (f32[8,2,64,512]{3,2,1,0:T(8,128)}, f32[8,2,64,512]{3,2,1,0:T(8,128)}, u32[]{:S(2)}, u32[]{:S(2)}) collective-permute-start(f32[8,2,64,512]{3,2,1,0:T(8,128)} %get-tuple-element.37), channel_id=1, source_target_pairs={{0,4},{1,5},{2,6},{3,7},{4,0},{5,1},{6,2},{7,3},{8,12},{9,13},{10,... | collective-permute-start | bytes 6291464 | tf_op jit(solution)/shard_map/ppermute | solution.py:127
  81.0 179.0 %collective-permute-start.4 = (f32[8,2,64,512]{3,2,1,0:T(8,128)}, f32[8,2,64,512]{3,2,1,0:T(8,128)}, u32[]{:S(2)}, u32[]{:S(2)}) collective-permute-start(f32[8,2,64,512]{3,2,1,0:T(8,128)} %get-tuple-element.36), channel_id=1, source_target_pairs={{0,5},{1,4},{2,7},{3,6},{4,1},{5,0},{6,3},{7,2},{8,13},{9,12},{10,... | collective-permute-start | bytes 6291464 | tf_op jit(solution)/shard_map/ppermute | solution.py:127
  84.9 178.3 %collective-permute-start.5 = (f32[8,2,64,512]{3,2,1,0:T(8,128)}, f32[8,2,64,512]{3,2,1,0:T(8,128)}, u32[]{:S(2)}, u32[]{:S(2)}) collective-permute-start(f32[8,2,64,512]{3,2,1,0:T(8,128)} %get-tuple-element.35), channel_id=1, source_target_pairs={{0,6},{1,7},{2,4},{3,5},{4,2},{5,3},{6,0},{7,1},{8,14},{9,15},{10,... | collective-permute-start | bytes 6291464 | tf_op jit(solution)/shard_map/ppermute | solution.py:127
  86.3 405.1 %all-to-all-start.3 = ((f32[2,8,32,4]{1,3,0,2:T(4,128)}), f32[2,8,32,4]{1,3,0,2:T(4,128)S(1)}, u32[]{:S(2)}, u32[]{:S(2)}) async-start(f32[2,8,32,4]{1,3,0,2:T(4,128)} %copy.86), calls=%async_computation.3 | async-start | bytes 262144 | tf_op jit(solution)/shard_map/all_to_all | solution.py:114
  120.1 146.2 %collective-permute-start.6 = (f32[8,2,64,512]{3,2,1,0:T(8,128)S(1)}, f32[8,2,64,512]{3,2,1,0:T(8,128)S(1)}, u32[]{:S(2)}, u32[]{:S(2)}) collective-permute-start(f32[8,2,64,512]{3,2,1,0:T(8,128)S(1)} %get-tuple-element.34), channel_id=1, source_target_pairs={{0,7},{1,6},{2,5},{3,4},{4,3},{5,2},{6,1},{7,0},{8,15},{9,14},{10,... | collective-permute-start | bytes 6291464 | tf_op jit(solution)/shard_map/ppermute | solution.py:127
  330.7 6.6 copy-start
  330.7 6.6 copy-start.1
  491.3 376.7 %all-to-all-start.2 = ((f32[2,1,32,65536]{3,0,1,2:T(2,128)}), f32[2,1,32,65536]{3,0,1,2:T(2,128)}, u32[]{:S(2)}, u32[]{:S(2)}) async-start(f32[2,1,32,65536]{3,0,1,2:T(2,128)} %copy.80), calls=%async_computation.2 | async-start | bytes 33554432 | tf_op jit(solution)/shard_map/all_to_all | solution.py:151
